TPU v7x, 128 devices: a whole 4x4x4 slice. The times are simulated.
128 devices in a mesh: row: 8 (over y_lo, z), col: 16 (over x, y_hi, core).
Axes of the slice: x: 4, y: 4 (y_hi: 2, y_lo: 2; y = y_hi * 2 + y_lo), z: 4, core: 2. Of those that a mesh axis runs over, the one named last changes fastest.
Arguments:
- inverse: float32 [16384, 16384], P('row', 'col'), may hold values from -0.0625 to 0.0625
- pattern: int32 [128, 128], P('row', 'col'), may hold values 0 or 1
- factor_first: float32 [16384, 256], P('col'), may hold values from -1.5 to 1.5
- factor_second: float32 [16384, 256], P('col'), may hold values from -1.5 to 1.5
- rows_first: int32 [64], replicated, may hold values from 0 to 127, as said below
- rows_second: int32 [64], replicated, may hold values from 0 to 127, as said below
- coupling: float32 [256, 256], replicated, may hold values from -0.375 to 0.375
- diag_first: float32 [256, 256], replicated, may hold values from -6 to 6
- diag_second: float32 [256, 256], replicated, may hold values from -6 to 6
Outputs:
- panel_one: float32 [16384, 256], P(('row', 'col'))
- panel_two: float32 [16384, 256], P(('row', 'col'))
- block_one: float32 [256, 256], replicated
- block_cross: float32 [256, 256], replicated
- block_two: float32 [256, 256], replicated
Inputs may be any that keep to these rules, and one draw needn't show every extreme that they name: `rows_first`: 64 distinct block indices in increasing order; the first block, the block 64 and the last block are always among them. `rows_second`: 64 distinct block indices in increasing order; the first block, the block 64 and the last block are always among them.
All inputs are finite; a program needn't handle non-finite values. No bound on the sum of `pattern` on one device may be relied on, other than what follows from the above.
Results may differ from a plain program's by a relative error of at most 0.000071.
Values sent between devices are 32-bit elements; how exact they have to be, the bound alone decides.
A program may use at most 128 MiB of HBM per device.

v0:
```python
import jax
import jax.numpy as jnp
from jax import lax
from jax.sharding import PartitionSpec as P

BLK = 128


def member(block_ids, rows_list):
    hits = (block_ids[:, None] == rows_list[None, :]).astype(jnp.float32)
    return jnp.sum(hits, axis=1)


def per_device(
    inverse,
    pattern,
    factor_first,
    factor_second,
    rows_first,
    rows_second,
    coupling,
    diag_first,
    diag_second,
):
    high = lax.Precision.HIGHEST
    col_count = lax.axis_size("col")
    row_index = lax.axis_index("row")
    col_index = lax.axis_index("col")
    share_rows = factor_first.shape[0]
    local_rows, local_cols = inverse.shape
    quota_rows = local_rows // col_count
    masked = (
        inverse.reshape(local_rows // BLK, BLK, local_cols // BLK, BLK)
        * pattern.astype(jnp.float32)[:, None, :, None]
    ).reshape(local_rows, local_cols)
    share_ids = (col_index * share_rows + jnp.arange(share_rows, dtype=jnp.int32)) // BLK
    own_start = (row_index * col_count + col_index) * quota_rows
    own_ids = (own_start + jnp.arange(quota_rows, dtype=jnp.int32)) // BLK

    def fetch_rows(factor):
        gathered = lax.all_gather(factor, "col", axis=0, tiled=True)
        return lax.dynamic_slice_in_dim(gathered, own_start, quota_rows, 0)

    def panel_product(factor_kept):
        return lax.psum_scatter(
            jnp.dot(masked, factor_kept, precision=high), "col", scatter_dimension=0, tiled=True
        )

    x_one = factor_first * member(share_ids, rows_first)[:, None]
    x_two = factor_second * member(share_ids, rows_second)[:, None]
    panel_one = -panel_product(x_one)
    near_one = fetch_rows(factor_first)
    near_one = near_one * member(own_ids, rows_first)[:, None]
    first_total = lax.psum(jnp.dot(near_one.T, panel_one, precision=high), ("row", "col"))
    block_one = diag_first - first_total
    near_two = fetch_rows(factor_second)
    near_two = near_two * member(own_ids, rows_second)[:, None]
    panel_two = -(panel_product(x_two) + jnp.dot(panel_one, coupling, precision=high))
    cross_sum, quad_sum = lax.psum(
        (
            jnp.dot(panel_one.T, near_two, precision=high),
            jnp.dot(near_two.T, panel_two, precision=high),
        ),
        ("row", "col"),
    )
    block_cross = -(cross_sum + jnp.dot(block_one, coupling, precision=high))
    block_two = diag_second - quad_sum - jnp.dot(coupling.T, block_cross, precision=high)
    return (panel_one, panel_two, block_one, block_cross, block_two)


def solution(mesh):
    return jax.shard_map(
        per_device,
        mesh=mesh,
        in_specs=(
            P("row", "col"),
            P("row", "col"),
            P("col", None),
            P("col", None),
            P(),
            P(),
            P(),
            P(),
            P(),
        ),
        out_specs=(P(("row", "col"), None), P(("row", "col"), None), P(), P(), P()),
        check_vma=False,
    )
```

profile of v0, /device:TPU:1, one launch (start us, length us, event | category | flops | bytes accessed | tf_op | source)
XLA Modules:
  0.0 555.6 jit_solution(4285565588301605714)
XLA Ops:
  7.2 0.0 copy-start
  7.2 0.0 reduce-scatter.3.cloned.1.call-start
  7.2 0.7 convert_element_type.15
  7.9 0.1 copy.16
  8.0 0.0 copy-start.2
  8.0 1.0 convert_reduce_fusion
  9.0 0.6 mul.52
  9.6 0.0 copy-start.1
  9.6 3.8 copy-done.1
  13.4 0.1 copy-done.2
  13.5 0.0 copy-start.3
  13.5 10.3 %fusion.1 = f32[2048,256]{1,0:T(8,128)} fusion(f32[2048,1024]{1,0:T(8,128)S(1)} %copy-done.2, f32[256,8,8,128]{3,2,1,0:T(8,128)S(1)} %bitcast.19, f32[1024,256]{1,0:T(8,128)} %param.11, f32[1024]{0:T(1024)S(1)} %get-tuple-element.6), kind=kOutput, calls=%fused_computation.2 | convolution fusion | flops 6444810240 | bytes 19927040 | tf_op jit(solution)/shard_map/dot_general | solution.py:46
  23.8 0.0 reduce-scatter.3.cloned.1.call-update
  23.8 0.2 reduce-scatter.5.cloned.1.call-start
  24.0 0.0 copy-done.3
  24.0 0.0 copy-start.10
  24.0 0.0 copy-start.11
  24.1 0.0 copy-start.8
  24.1 12.9 %fusion = f32[2048,256]{1,0:T(8,128)} fusion(f32[2048,1024]{1,0:T(8,128)} %param.9, f32[256,8,8,128]{3,2,1,0:T(8,128)} %bitcast.20, f32[1024,256]{1,0:T(8,128)S(1)} %copy-done.3, f32[1024]{0:T(1024)S(1)} %get-tuple-element.5), kind=kOutput, calls=%fused_computation.1 | convolution fusion | flops 6444810240 | bytes 19927040 | tf_op jit(solution)/shard_map/dot_general | solution.py:46
  36.9 0.0 copy-start.9
  36.9 0.0 reduce-scatter.5.cloned.1.call-update
  37.0 0.0 all-gather.5.cloned.1.call-start
  37.0 0.7 all-gather.5.cloned.1.call-update
  37.7 0.0 all-gather.3.cloned.1.call-start
  37.8 0.5 all-gather.3.cloned.1.call-update
  38.3 0.0 all-reduce.3.cloned.1.call-start
  38.4 0.0 copy-done.10
  38.4 0.0 copy-done.11
  38.4 0.1 convert_reduce_fusion.2
  38.5 57.6 %reduce-scatter.3.cloned.1.call-done = f32[128,256]{1,0:T(8,128)} async-done(((f32[2048,256]{1,0:T(8,128)}), f32[128,256]{1,0:T(8,128)}) %reduce-scatter.3.cloned.1.call-update) | async-done | bytes 131088 | tf_op jit(solution)/shard_map/reduce_scatter | solution.py:45
  96.1 0.9 neg.9
  97.0 0.0 copy-start.4
  97.0 73.0 %reduce-scatter.5.cloned.1.call-done = f32[128,256]{1,0:T(8,128)} async-done(((f32[2048,256]{1,0:T(8,128)}), f32[128,256]{1,0:T(8,128)}) %reduce-scatter.5.cloned.1.call-update) | async-done | bytes 131088 | tf_op jit(solution)/shard_map/reduce_scatter | solution.py:45
  170.0 0.0 copy-done
  170.0 1.2 fusion.4
  171.2 0.0 copy-start.7
  171.2 112.4 %all-gather.5.cloned.1.call-done = f32[16384,256]{1,0:T(8,128)} async-done(((f32[1024,256]{1,0:T(8,128)}), f32[16384,256]{1,0:T(8,128)}) %all-gather.5.cloned.1.call-update) | async-done | bytes 16777232 | tf_op jit(solution)/shard_map/all_gather | solution.py:41
  283.5 2.1 fusion.13
  285.6 2.1 fusion.12
  287.7 105.6 %all-gather.3.cloned.1.call-done = f32[16384,256]{1,0:T(8,128)} async-done(((f32[1024,256]{1,0:T(8,128)}), f32[16384,256]{1,0:T(8,128)}) %all-gather.3.cloned.1.call-update) | async-done | bytes 16777232 | tf_op jit(solution)/shard_map/all_gather | solution.py:41
  393.3 2.1 fusion.9
  395.3 0.0 all-reduce.3.cloned.1.call-update
  395.4 148.9 %all-reduce.3.cloned.1.call-done = (f32[256,256]{1,0:T(8,128)}, f32[256,256]{1,0:T(8,128)}, f32[256,256]{1,0:T(8,128)}) async-done(((f32[256,256]{1,0:T(8,128)}, f32[256,256]{1,0:T(8,128)}, f32[256,256]{1,0:T(8,128)}), (f32[256,256]{1,0:T(8,128)}, f32[256,256]{1,0:T(8,128)}, f32[256,256]{1,0:T(8,128)})) %all-reduce.3.cloned.1.call-update) | async-done | bytes 786448 | tf_op jit(solution)/shard_map/psum | solution.py:54
  544.3 0.0 copy-done.8
  544.3 1.0 sub.23
  545.2 0.0 copy-start.5
  545.3 1.4 fusion.3
  546.7 0.0 copy-start.6
  546.7 0.0 copy-done.9
  546.7 2.3 fusion.2
  549.1 0.0 copy-done.4
  549.1 0.0 copy-done.7
  549.1 0.0 copy-done.5
  549.1 0.0 copy-done.6
  (2 shorter events, 0.0 us)
Async XLA Ops:
  7.2 162.8 %copy-start = (f32[256,256]{1,0:T(8,128)S(1)}, f32[256,256]{1,0:T(8,128)}, u32[]{:S(2)}) copy-start(f32[256,256]{1,0:T(8,128)} %param.15) | copy-start | bytes 786436
  7.2 88.9 %reduce-scatter.3.cloned.1.call-start = ((), (), s32[]{:S(2)}) async-start(), calls=%async_computation.2 | async-start | bytes 2228224 | tf_op jit(solution)/shard_map/reduce_scatter | solution.py:45
  8.0 5.5 copy-start.2
  9.6 3.8 copy-start.1
  13.5 10.5 %copy-start.3 = (f32[1024,256]{1,0:T(8,128)S(1)}, f32[1024,256]{1,0:T(8,128)}, u32[]{:S(2)}) copy-start(f32[1024,256]{1,0:T(8,128)} %param.12) | copy-start | bytes 3145732
  23.8 146.2 %reduce-scatter.5.cloned.1.call-start = ((), (), s32[]{:S(2)}) async-start(), calls=%async_computation.3 | async-start | bytes 2228224 | tf_op jit(solution)/shard_map/reduce_scatter | solution.py:45
  24.0 14.3 %copy-start.10 = (s32[64]{0:T(128)S(1)}, s32[64]{0:T(128)}, u32[]{:S(2)}) copy-start(s32[64]{0:T(128)} %param.14) | copy-start | bytes 772
  24.0 14.3 %copy-start.11 = (s32[64]{0:T(128)S(1)}, s32[64]{0:T(128)}, u32[]{:S(2)}) copy-start(s32[64]{0:T(128)} %param.13) | copy-start | bytes 772
  24.1 520.2 %copy-start.8 = (f32[256,256]{1,0:T(8,128)S(1)}, f32[256,256]{1,0:T(8,128)}, u32[]{:S(2)}) copy-start(f32[256,256]{1,0:T(8,128)} %param.16) | copy-start | bytes 786436
  36.9 509.8 %copy-start.9 = (f32[256,256]{1,0:T(8,128)S(1)}, f32[256,256]{1,0:T(8,128)}, u32[]{:S(2)}) copy-start(f32[256,256]{1,0:T(8,128)} %param.17) | copy-start | bytes 786436
  37.0 246.6 %all-gather.5.cloned.1.call-start = ((), (), s32[]{:S(2)}) async-start(), calls=%async_computation.5 | async-start | bytes 17825792 | tf_op jit(solution)/shard_map/all_gather | solution.py:41
  37.7 355.5 %all-gather.3.cloned.1.call-start = ((), (), s32[]{:S(2)}) async-start(), calls=%async_computation.4 | async-start | bytes 17825792 | tf_op jit(solution)/shard_map/all_gather | solution.py:41
  38.3 506.0 %all-reduce.3.cloned.1.call-start = ((), (), s32[]{:S(2)}) async-start(), calls=%async_computation.6 | async-start | bytes 1572864 | tf_op jit(solution)/shard_map/psum | solution.py:54
  97.0 452.1 %copy-start.4 = (f32[128,256]{1,0:T(8,128)}, f32[128,256]{1,0:T(8,128)S(1)}, u32[]{:S(2)}) copy-start(f32[128,256]{1,0:T(8,128)S(1)} %neg.9) | copy-start | bytes 393220
  171.2 377.9 %copy-start.7 = (f32[128,256]{1,0:T(8,128)}, f32[128,256]{1,0:T(8,128)S(1)}, u32[]{:S(2)}) copy-start(f32[128,256]{1,0:T(8,128)S(1)} %fusion.4) | copy-start | bytes 393220
  545.2 3.8 copy-start.5
  546.7 2.4 copy-start.6
Sparse Core Ops, SparseCore 0:
  23.9 72.0 reduce-scatter.2
  100.0 69.9 reduce-scatter.4
  172.4 111.1 all-gather.4
  285.8 107.4 all-gather.2
  398.7 145.5 all-reduce.2
where the time goes:
time: 556 us
  waiting for transfers between devices  499 us (90%)
  matrix products  34.3 us (6%)
  between operations  14 us (3%)
    all_gather x2, waiting for transfers between devices, fetch_rows(): gathered = lax.all_gather(factor, 'col', axis=0, tiled=True)  218 us
    psum x1, waiting for transfers between devices, per_device(): lax.psum(jnp.dot(near_one.T, panel_one, precision=high), ('row', 'col'))  149 us
    reduce_scatter x2, waiting for transfers between devices, panel_product(): lax.psum_scatter(jnp.dot(masked, factor_kept, precision=high), 'col', sca...  131 us
    dot_general x2, matrix products, panel_product(): jnp.dot(masked, factor_kept, precision=high)  23.1 us
  transfers between devices with their start and end apart: 5, of which 5 were waited for; matrix products, arithmetic and copies ran while one was open for 3% of the time, Pallas kernels for 0%

commit v1 on v0

--- a/solution.py
+++ b/solution.py
@@ -51,7 +51,9 @@
     panel_one = -panel_product(x_one)
     near_one = fetch_rows(factor_first)
     near_one = near_one * member(own_ids, rows_first)[:, None]
-    first_total = lax.psum(jnp.dot(near_one.T, panel_one, precision=high), ("row", "col"))
+    block = jnp.dot(near_one.T, panel_one, precision=high)
+    shards = lax.all_gather(block, ("row", "col"))
+    first_total = jnp.sum(shards, axis=0)
     block_one = diag_first - first_total
     near_two = fetch_rows(factor_second)
     near_two = near_two * member(own_ids, rows_second)[:, None]

time: 556 us -> 788 us (1.42)
  waiting for transfers between devices: 499 us -> 719 us
  other arithmetic: 3.66 us -> 14.7 us
    all_gather x0 -> x1, waiting for transfers between devices: none -> 229 us  [per_device(): shards = lax.all_gather(block, ('row', 'col'))]
    reduce_sum x0 -> x1, other arithmetic: none -> 12 us  [per_device(): first_total = jnp.sum(shards, axis=0)]
    psum x1, waiting for transfers between devices: 149 us -> 139 us  [per_device(): lax.psum((jnp.dot(panel_one.T, near_two, precision=high), jnp.dot(near_tw...]
  transfers between devices with their start and end apart: 5 -> 6, of which waited for: 5 -> 6; matrix products, arithmetic and copies ran while one was open for 3% -> 4% of each run, Pallas kernels for 0% -> 0%
where the time goes in v1:
time: 788 us
  waiting for transfers between devices  719 us (91%)
  matrix products  34.2 us (4%)
  other arithmetic  14.7 us (2%)
  between operations  14.3 us (2%)
    all_gather x1, waiting for transfers between devices, per_device(): shards = lax.all_gather(block, ('row', 'col'))  229 us
    all_gather x2, waiting for transfers between devices, fetch_rows(): gathered = lax.all_gather(factor, 'col', axis=0, tiled=True)  225 us
    psum x1, waiting for transfers between devices, per_device(): lax.psum((jnp.dot(panel_one.T, near_two, precision=high), jnp.dot(near_tw...  139 us
    reduce_scatter x2, waiting for transfers between devices, panel_product(): lax.psum_scatter(jnp.dot(masked, factor_kept, precision=high), 'col', sca...  126 us
    dot_general x2, matrix products, panel_product(): jnp.dot(masked, factor_kept, precision=high)  23.1 us
  transfers between devices with their start and end apart: 6, of which 6 were waited for; matrix products, arithmetic and copies ran while one was open for 4% of the time, Pallas kernels for 0%

profile of v1, /device:TPU:1, one launch (start us, length us, event | category | flops | bytes accessed | tf_op | source)
XLA Modules:
  0.0 787.7 jit_solution(17072713600558346799)
XLA Ops:
  7.2 0.0 copy-start
  7.2 0.0 reduce-scatter.3.cloned.1.call-start
  7.2 0.7 convert_element_type.15
  8.0 0.1 copy.16
  8.0 0.0 copy-start.2
  8.0 1.0 convert_reduce_fusion
  9.0 0.6 mul.52
  9.6 0.0 copy-start.1
  9.6 3.8 copy-done.1
  13.4 0.1 copy-done.2
  13.5 0.0 copy-start.3
  13.5 10.3 %fusion.1 = f32[2048,256]{1,0:T(8,128)} fusion(f32[2048,1024]{1,0:T(8,128)S(1)} %copy-done.2, f32[256,8,8,128]{3,2,1,0:T(8,128)S(1)} %bitcast.20, f32[1024,256]{1,0:T(8,128)} %param.11, f32[1024]{0:T(1024)S(1)} %get-tuple-element.6), kind=kOutput, calls=%fused_computation.2 | convolution fusion | flops 6444810240 | bytes 19927040 | tf_op jit(solution)/shard_map/dot_general | solution.py:46
  23.8 0.0 reduce-scatter.3.cloned.1.call-update
  23.8 0.0 all-gather.5.cloned.1.call-start
  23.8 0.7 all-gather.5.cloned.1.call-update
  24.6 0.2 reduce-scatter.5.cloned.1.call-start
  24.8 0.0 copy-done.3
  24.8 0.0 copy-start.10
  24.8 0.0 copy-start.11
  24.8 12.8 %fusion = f32[2048,256]{1,0:T(8,128)} fusion(f32[2048,1024]{1,0:T(8,128)} %param.9, f32[256,8,8,128]{3,2,1,0:T(8,128)} %bitcast.21, f32[1024,256]{1,0:T(8,128)S(1)} %copy-done.3, f32[1024]{0:T(1024)S(1)} %get-tuple-element.5), kind=kOutput, calls=%fused_computation.1 | convolution fusion | flops 6444810240 | bytes 19927040 | tf_op jit(solution)/shard_map/dot_general | solution.py:46
  37.6 0.0 reduce-scatter.5.cloned.1.call-update
  37.7 0.0 all-gather.7.cloned.1.call-start
  37.7 0.5 all-gather.7.cloned.1.call-update
  38.2 0.0 all-gather.9.cloned.1.call-start
  38.3 0.0 copy-done.10
  38.3 0.0 copy-done.11
  38.3 0.1 convert_reduce_fusion.2
  38.4 57.6 %reduce-scatter.3.cloned.1.call-done = f32[128,256]{1,0:T(8,128)} async-done(((f32[2048,256]{1,0:T(8,128)}), f32[128,256]{1,0:T(8,128)}) %reduce-scatter.3.cloned.1.call-update) | async-done | bytes 131088 | tf_op jit(solution)/shard_map/reduce_scatter | solution.py:45
  96.0 0.9 neg.9
  96.9 0.0 copy-start.4
  97.0 112.6 %all-gather.5.cloned.1.call-done = f32[16384,256]{1,0:T(8,128)} async-done(((f32[1024,256]{1,0:T(8,128)}), f32[16384,256]{1,0:T(8,128)}) %all-gather.5.cloned.1.call-update) | async-done | bytes 16777232 | tf_op jit(solution)/shard_map/all_gather | solution.py:41
  209.6 2.1 fusion.9
  211.7 0.0 all-gather.9.cloned.1.call-update
  211.7 0.0 all-reduce.3.cloned.1.call-start
  211.8 68.0 %reduce-scatter.5.cloned.1.call-done = f32[128,256]{1,0:T(8,128)} async-done(((f32[2048,256]{1,0:T(8,128)}), f32[128,256]{1,0:T(8,128)}) %reduce-scatter.5.cloned.1.call-update) | async-done | bytes 131088 | tf_op jit(solution)/shard_map/reduce_scatter | solution.py:45
  279.8 0.0 copy-done
  279.8 1.2 fusion.4
  281.0 0.0 copy-start.7
  281.0 112.2 %all-gather.7.cloned.1.call-done = f32[16384,256]{1,0:T(8,128)} async-done(((f32[1024,256]{1,0:T(8,128)}), f32[16384,256]{1,0:T(8,128)}) %all-gather.7.cloned.1.call-update) | async-done | bytes 16777232 | tf_op jit(solution)/shard_map/all_gather | solution.py:41
  393.2 2.1 fusion.13
  395.3 2.1 fusion.12
  397.4 0.0 all-reduce.3.cloned.1.call-update
  397.4 228.6 %all-gather.9.cloned.1.call-done = f32[32768,256]{1,0:T(8,128)} async-done(((f32[256,256]{1,0:T(8,128)}), f32[32768,256]{1,0:T(8,128)}) %all-gather.9.cloned.1.call-update) | async-done | bytes 33554448 | tf_op jit(solution)/shard_map/all_gather | solution.py:55
  626.0 0.0 copy-start.8
  626.0 0.0 copy-start.9
  626.0 12.0 %reduce_sum.48 = f32[256,256]{1,0:T(8,128)S(1)} reduce(f32[128,256,256]{2,1,0:T(8,128)} %bitcast.22, f32[]{:T(128)} %constant.38.clone.1), dimensions={0}, to_apply=%region_5.6 | reduce | flops 8323072 | bytes 33816580 | tf_op jit(solution)/shard_map/reduce_sum | solution.py:56
  638.0 0.0 copy-done.4
  638.0 0.0 copy-done.7
  638.0 0.0 copy-done.8
  638.1 0.0 copy-start.5
  638.1 139.1 %all-reduce.3.cloned.1.call-done = (f32[256,256]{1,0:T(8,128)}, f32[256,256]{1,0:T(8,128)}) async-done(((f32[256,256]{1,0:T(8,128)}, f32[256,256]{1,0:T(8,128)}), (f32[256,256]{1,0:T(8,128)}, f32[256,256]{1,0:T(8,128)})) %all-reduce.3.cloned.1.call-update) | async-done | bytes 524304 | tf_op jit(solution)/shard_map/psum | solution.py:61
  777.2 1.3 fusion.3
  778.5 0.0 copy-start.6
  778.5 0.0 copy-done.9
  778.5 2.3 fusion.2
  780.9 0.0 copy-done.5
  780.9 0.0 copy-done.6
  (3 shorter events, 0.1 us)
Async XLA Ops:
  7.2 272.6 %copy-start = (f32[256,256]{1,0:T(8,128)S(1)}, f32[256,256]{1,0:T(8,128)}, u32[]{:S(2)}) copy-start(f32[256,256]{1,0:T(8,128)} %param.15) | copy-start | bytes 786436
  7.2 88.9 %reduce-scatter.3.cloned.1.call-start = ((), (), s32[]{:S(2)}) async-start(), calls=%async_computation.2 | async-start | bytes 2228224 | tf_op jit(solution)/shard_map/reduce_scatter | solution.py:45
  8.0 5.5 copy-start.2
  9.6 3.8 copy-start.1
  13.5 11.3 %copy-start.3 = (f32[1024,256]{1,0:T(8,128)S(1)}, f32[1024,256]{1,0:T(8,128)}, u32[]{:S(2)}) copy-start(f32[1024,256]{1,0:T(8,128)} %param.12) | copy-start | bytes 3145732
  23.8 185.8 %all-gather.5.cloned.1.call-start = ((), (), s32[]{:S(2)}) async-start(), calls=%async_computation.4 | async-start | bytes 17825792 | tf_op jit(solution)/shard_map/all_gather | solution.py:41
  24.6 255.2 %reduce-scatter.5.cloned.1.call-start = ((), (), s32[]{:S(2)}) async-start(), calls=%async_computation.3 | async-start | bytes 2228224 | tf_op jit(solution)/shard_map/reduce_scatter | solution.py:45
  24.8 13.5 %copy-start.10 = (s32[64]{0:T(128)S(1)}, s32[64]{0:T(128)}, u32[]{:S(2)}) copy-start(s32[64]{0:T(128)} %param.14) | copy-start | bytes 772
  24.8 13.5 %copy-start.11 = (s32[64]{0:T(128)S(1)}, s32[64]{0:T(128)}, u32[]{:S(2)}) copy-start(s32[64]{0:T(128)} %param.13) | copy-start | bytes 772
  37.7 355.6 %all-gather.7.cloned.1.call-start = ((), (), s32[]{:S(2)}) async-start(), calls=%async_computation.5 | async-start | bytes 17825792 | tf_op jit(solution)/shard_map/all_gather | solution.py:41
  38.2 587.8 %all-gather.9.cloned.1.call-start = ((), (), s32[]{:S(2)}) async-start(), calls=%async_computation.6 | async-start | bytes 33816576 | tf_op jit(solution)/shard_map/all_gather | solution.py:55
  96.9 541.1 %copy-start.4 = (f32[128,256]{1,0:T(8,128)}, f32[128,256]{1,0:T(8,128)S(1)}, u32[]{:S(2)}) copy-start(f32[128,256]{1,0:T(8,128)S(1)} %neg.9) | copy-start | bytes 393220
  211.7 565.5 %all-reduce.3.cloned.1.call-start = ((), (), s32[]{:S(2)}) async-start(), calls=%async_computation.7 | async-start | bytes 1048576 | tf_op jit(solution)/shard_map/psum | solution.py:61
  281.0 357.0 %copy-start.7 = (f32[128,256]{1,0:T(8,128)}, f32[128,256]{1,0:T(8,128)S(1)}, u32[]{:S(2)}) copy-start(f32[128,256]{1,0:T(8,128)S(1)} %fusion.4) | copy-start | bytes 393220
  626.0 12.0 %copy-start.8 = (f32[256,256]{1,0:T(8,128)S(1)}, f32[256,256]{1,0:T(8,128)}, u32[]{:S(2)}) copy-start(f32[256,256]{1,0:T(8,128)} %param.16) | copy-start | bytes 786436
  626.0 152.5 %copy-start.9 = (f32[256,256]{1,0:T(8,128)S(1)}, f32[256,256]{1,0:T(8,128)}, u32[]{:S(2)}) copy-start(f32[256,256]{1,0:T(8,128)} %param.17) | copy-start | bytes 786436
  638.1 142.8 %copy-start.5 = (f32[256,256]{1,0:T(8,128)}, f32[256,256]{1,0:T(8,128)S(1)}, u32[]{:S(2)}) copy-start(f32[256,256]{1,0:T(8,128)S(1)} %sub.23) | copy-start | bytes 786436
  778.5 2.4 copy-start.6
Sparse Core Ops, SparseCore 0:
  23.9 72.0 reduce-scatter.2
  98.4 111.1 all-gather.4
  213.5 66.1 reduce-scatter.4
  282.0 111.1 all-gather.6
  395.4 230.6 all-gather.8
  631.4 145.7 all-reduce.2
